TPU v7x, 256 devices: a whole 4x4x8 slice. The times are simulated.
256 devices in a mesh: ctx: 32 (over z, x), tp: 8 (over y, core).
Axes of the slice: x: 4, y: 4, z: 8, core: 2. Of those that a mesh axis runs over, the one named last changes fastest.
Arguments:
- tokens: bfloat16 [24576, 4096], P('ctx'), may hold values from -6 to 6
- qkv_weight: bfloat16 [3, 4096, 4096], P(None, 'ctx', 'tp'), may hold values from -0.09375 to 0.09375
- short_filter: float32 [3, 7, 4096], P(None, None, 'tp'), may hold values from -2.4 to 2.4
- long_filter: float32 [256, 128], P('tp'), may hold values from -0.9 to 0.9
- decay_rate: float32 [256], P('tp'), may hold values from 0.004 to 0.2
- skip_gain: float32 [4096], P('tp'), may hold values from -3 to 3
- out_weight: bfloat16 [4096, 4096], P('tp', 'ctx'), may hold values from -0.09375 to 0.09375
Outputs:
- block_out: bfloat16 [24576, 4096], P(('ctx', 'tp'))
All inputs are finite; a program needn't handle non-finite values.
Results may differ from a plain program's by a relative error of at most 0.008.
Values may be sent and summed in bfloat16 or wider, within the bound.
A program may use at most 64 MiB of HBM per device.

v0:
```python
import jax
import jax.numpy as jnp
from jax import lax
from jax.sharding import PartitionSpec as P


def short_conv(extended, short_filter):
    span = short_filter.shape[1]
    length = extended.shape[2] - (span - 1)
    result = short_filter[:, 0, :, None] * extended[:, :, span - 1 :]
    for offset in range(1, span):
        start = span - 1 - offset
        result = result + short_filter[:, offset, :, None] * extended[:, :, start : start + length]
    return result


def banded(filters):
    tap_count = filters.shape[1]
    row_index = jnp.arange(tap_count)[:, None]
    col_index = jnp.arange(tap_count)[None, :]
    distance = (row_index - col_index) % tap_count
    picker = (distance[None, :, :] == jnp.arange(tap_count)[:, None, None]).astype(jnp.bfloat16)
    full_band = jnp.einsum("gk,kij->gij", filters, picker, preferred_element_type=jnp.float32)
    lower_part = row_index >= col_index
    lower_band = jnp.where(lower_part[None], full_band, 0.0).astype(jnp.bfloat16)
    upper_band = jnp.where(lower_part[None], 0.0, full_band).astype(jnp.bfloat16)
    return (lower_band, upper_band)


def long_mix(features, gated, previous, filters, gain):
    channel_count, length = gated.shape
    tap_count = filters.shape[1]
    group_count = filters.shape[0]
    extended = jnp.concatenate([previous, gated], axis=1)
    blocks = extended.reshape(
        group_count, channel_count // group_count, length // tap_count + 1, tap_count
    )
    lower_band, upper_band = banded(filters)
    current = jnp.einsum(
        "gij,gcbj->gcbi", lower_band, blocks[:, :, 1:], preferred_element_type=jnp.float32
    )
    current = current + jnp.einsum(
        "gij,gcbj->gcbi", upper_band, blocks[:, :, :-1], preferred_element_type=jnp.float32
    )
    filtered = current.reshape(channel_count, length)
    return (features[0] * (filtered + gain[:, None] * gated.astype(jnp.float32))).astype(
        jnp.bfloat16
    )


def per_device(tokens, qkv_weight, short_filter, long_filter, decay_rate, skip_gain, out_weight):
    local_width = qkv_weight.shape[2]
    tap_count = long_filter.shape[1]
    span = short_filter.shape[1]
    group_width = local_width // long_filter.shape[0]
    projected = jnp.einsum(
        "tr,src->sct",
        tokens,
        lax.all_gather(qkv_weight, "ctx", axis=1, tiled=True),
        preferred_element_type=jnp.float32,
    )
    qkv = projected.astype(jnp.bfloat16)
    tap_index = jnp.arange(tap_count, dtype=jnp.float32)
    filters = (long_filter * jnp.exp(-decay_rate[:, None] * tap_index[None, :])).astype(
        jnp.bfloat16
    )
    moved = lax.all_to_all(qkv, "ctx", split_axis=1, concat_axis=2, tiled=True)
    share = moved.shape[1]
    position = lax.axis_index("ctx")
    part_short = lax.dynamic_slice_in_dim(short_filter, position * share, share, 2)
    part_filters = lax.dynamic_slice_in_dim(
        filters, position * (share // group_width), share // group_width, 0
    )
    part_gain = lax.dynamic_slice_in_dim(skip_gain, position * share, share, 0)
    leading = jnp.zeros((3, share, span - 1), jnp.bfloat16)
    features = short_conv(jnp.concatenate([leading, moved], axis=2), part_short)
    gated = (features[1] * features[2]).astype(jnp.bfloat16)
    previous = jnp.zeros((share, tap_count), jnp.bfloat16)
    regrouped = long_mix(features, gated, previous, part_filters, part_gain)
    mixed = lax.all_to_all(regrouped, "ctx", split_axis=1, concat_axis=0, tiled=True)
    out_rows = lax.all_gather(out_weight, "ctx", axis=1, tiled=True)
    summed = lax.psum_scatter(
        lax.dot_general(
            mixed, out_rows, (((0,), (0,)), ((), ())), preferred_element_type=jnp.float32
        ),
        "tp",
        scatter_dimension=0,
        tiled=True,
    )
    return summed.astype(jnp.bfloat16)


def solution(mesh):
    in_specs = (
        P("ctx", None),
        P(None, "ctx", "tp"),
        P(None, None, "tp"),
        P("tp", None),
        P("tp"),
        P("tp"),
        P("tp", "ctx"),
    )
    out_specs = P(("ctx", "tp"), None)
    return jax.shard_map(
        per_device, mesh=mesh, in_specs=in_specs, out_specs=out_specs, check_vma=False
    )
```

profile of v0, /device:TPU:1, one launch (start us, length us, event | category | flops | bytes accessed | tf_op | source)
XLA Modules:
  0.0 379.6 jit_solution(5646571431311405019)
XLA Ops:
  6.5 0.0 all-gather.3.cloned.1.call-start
  6.5 1.9 copy.14
  8.5 0.0 all-gather.3.cloned.1.call-update
  8.5 127.2 %all-gather.3.cloned.1.call-done = bf16[3,4096,512]{1,2,0:T(8,128)(2,1)} async-done(((bf16[3,128,512]{1,2,0:T(8,128)(2,1)}), bf16[3,4096,512]{1,2,0:T(8,128)(2,1)}) %all-gather.3.cloned.1.call-update) | async-done | bytes 12582928 | tf_op jit(solution)/shard_map/all_gather | solution.py:59
  135.6 14.8 %fusion.4 = bf16[3,512,768]{2,1,0:T(8,128)(2,1)S(1)} fusion(bf16[3,4096,512]{1,2,0:T(8,128)(2,1)} %all-gather.3.cloned.1.call-done, bf16[768,4096]{1,0:T(8,128)(2,1)} %param.7), kind=kOutput, calls=%fused_computation.11 | convolution fusion | flops 9664856064 | bytes 21233664 | tf_op jit(solution)/shard_map/tr,src->sct/dot_general | solution.py:56
  150.4 3.7 copy.15
  154.1 0.0 copy-start.1
  154.1 6.8 %all-to-all-start = ((bf16[3,512,768]{2,0,1:T(4,128)(2,1)}), bf16[3,512,768]{2,0,1:T(4,128)(2,1)S(1)}, u32[]{:S(2)}, u32[]{:S(2)}) async-start(bf16[3,512,768]{2,0,1:T(4,128)(2,1)} %copy.15), calls=%async_computation | async-start | bytes 6291456 | tf_op jit(solution)/shard_map/all_to_all | solution.py:67
  160.9 0.2 all-gather.5.cloned.1.call-start
  161.1 0.5 all-gather.5.cloned.1.call-update
  161.6 1.1 constant_dynamic-slice_fusion.5
  162.7 0.0 copy-done.1
  162.7 0.8 dynamic_slice.11
  163.5 0.6 dynamic-slice.7
  164.1 1.2 iota_compare_fusion
  165.4 3.5 fusion
  168.8 66.1 %all-to-all-done = bf16[3,512,768]{2,0,1:T(4,128)(2,1)S(1)} async-done(((bf16[3,512,768]{2,0,1:T(4,128)(2,1)}), bf16[3,512,768]{2,0,1:T(4,128)(2,1)S(1)}, u32[]{:S(2)}, u32[]{:S(2)}) %all-to-all-start) | async-done | bytes 2359328 | tf_op jit(solution)/shard_map/all_to_all | solution.py:67
  234.9 3.1 copy.50
  238.0 3.0 all_to_all.28
  241.1 4.9 %multiply_add_fusion = f32[3,16,24576]{2,1,0:T(8,128)S(1)} fusion(bf16[3,16,24576]{2,1,0:T(8,128)(2,1)S(1)} %all_to_all.28, f32[3,16]{1,0:T(4,128)S(1)} %get-tuple-element.14, f32[3,16]{1,0:T(4,128)S(1)} %get-tuple-element.15, f32[3,16]{1,0:T(4,128)S(1)} %get-tuple-element.16, f32[3,16]{1,0:T(4,128)S(1)} %get-tuple-element.17, ...), kind=kLoop, calls=%fused_computation.5 | loop fusion | flops 23592960 | bytes 7079232 | tf_op jit(solution)/shard_map/add | solution.py:13
  245.9 0.2 fusion.7
  246.2 1.0 concatenate.7
  247.1 1.5 reshape.79
  248.7 0.4 fusion.9
  249.0 1.5 convolution_add_fusion
  250.6 2.6 reshape.83
  253.2 0.0 copy-start
  253.2 0.5 copy.29
  253.7 0.2 copy.30
  253.8 0.8 copy-done
  254.7 3.4 fusion.8
  258.0 6.4 %all-to-all-start.1 = ((bf16[16,32,768]{2,0,1:T(8,128)(2,1)}), bf16[16,32,768]{2,0,1:T(8,128)(2,1)S(1)}, u32[]{:S(2)}, u32[]{:S(2)}) async-start(bf16[16,32,768]{2,0,1:T(8,128)(2,1)} %fusion.8), calls=%async_computation.1 | async-start | bytes 1572864 | tf_op jit(solution)/shard_map/all_to_all | solution.py:80
  264.5 0.0 reduce-scatter.2.cloned.1.call-start
  264.5 7.9 %all-gather.5.cloned.1.call-done = bf16[512,4096]{1,0:T(8,128)(2,1)} async-done(((bf16[512,128]{1,0:T(8,128)(2,1)}), bf16[512,4096]{1,0:T(8,128)(2,1)}) %all-gather.5.cloned.1.call-update) | async-done | bytes 4194320 | tf_op jit(solution)/shard_map/all_gather | solution.py:81
  272.4 15.2 %all-to-all-done.1 = bf16[16,32,768]{2,0,1:T(8,128)(2,1)S(1)} async-done(((bf16[16,32,768]{2,0,1:T(8,128)(2,1)}), bf16[16,32,768]{2,0,1:T(8,128)(2,1)S(1)}, u32[]{:S(2)}, u32[]{:S(2)}) %all-to-all-start.1) | async-done | bytes 786464 | tf_op jit(solution)/shard_map/all_to_all | solution.py:80
  287.6 8.5 %fusion.29 = f32[768,4096]{1,0:T(8,128)} fusion(bf16[512,768]{1,0:T(8,128)(2,1)S(1)} %bitcast.66, bf16[512,4096]{1,0:T(8,128)(2,1)} %all-gather.5.cloned.1.call-done), kind=kOutput, calls=%fused_computation.59 | convolution fusion | flops 3221225472 | bytes 17563648 | tf_op jit(solution)/shard_map/dot_general | solution.py:83
  296.2 0.0 reduce-scatter.2.cloned.1.call-update
  296.2 74.5 %reduce-scatter.2.cloned.1.call-done = f32[96,4096]{1,0:T(8,128)} async-done(((f32[768,4096]{1,0:T(8,128)}), f32[96,4096]{1,0:T(8,128)}) %reduce-scatter.2.cloned.1.call-update) | async-done | bytes 1572880 | tf_op jit(solution)/shard_map/reduce_scatter | solution.py:82
  370.7 2.4 convert_element_type.74
  (6 shorter events, 0.1 us)
Async XLA Ops:
  6.5 129.1 %all-gather.3.cloned.1.call-start = ((), (), s32[]{:S(2)}) async-start(), calls=%async_computation.3 | async-start | bytes 12976128 | tf_op jit(solution)/shard_map/all_gather | solution.py:59
  154.1 8.6 %copy-start.1 = (f32[32]{0:T(128)S(1)}, f32[32]{0:T(128)}, u32[]{:S(2)}) copy-start(f32[32]{0:T(128)} %param.11) | copy-start | bytes 388
  154.1 80.8 %all-to-all-start = ((bf16[3,512,768]{2,0,1:T(4,128)(2,1)}), bf16[3,512,768]{2,0,1:T(4,128)(2,1)S(1)}, u32[]{:S(2)}, u32[]{:S(2)}) async-start(bf16[3,512,768]{2,0,1:T(4,128)(2,1)} %copy.15), calls=%async_computation | async-start | bytes 6291456 | tf_op jit(solution)/shard_map/all_to_all | solution.py:67
  160.9 111.6 %all-gather.5.cloned.1.call-start = ((), (), s32[]{:S(2)}) async-start(), calls=%async_computation.4 | async-start | bytes 4325376 | tf_op jit(solution)/shard_map/all_gather | solution.py:81
  253.2 1.5 copy-start
  258.0 29.6 %all-to-all-start.1 = ((bf16[16,32,768]{2,0,1:T(8,128)(2,1)}), bf16[16,32,768]{2,0,1:T(8,128)(2,1)S(1)}, u32[]{:S(2)}, u32[]{:S(2)}) async-start(bf16[16,32,768]{2,0,1:T(8,128)(2,1)} %fusion.8), calls=%async_computation.1 | async-start | bytes 1572864 | tf_op jit(solution)/shard_map/all_to_all | solution.py:80
  264.5 106.2 %reduce-scatter.2.cloned.1.call-start = ((), (), s32[]{:S(2)}) async-start(), calls=%async_computation.5 | async-start | bytes 14155776 | tf_op jit(solution)/shard_map/reduce_scatter | solution.py:82
Sparse Core Ops, SparseCore 0:
  9.8 125.8 all-gather.2
  164.1 108.2 all-gather.4
  296.3 74.2 reduce-scatter.1
where the time goes:
time: 380 us
  waiting for transfers between devices  291 us (77%)
  matrix products  28.7 us (8%)
  local copies, waits for them, and re-layouts  20.7 us (5%)
  starting transfers between devices  13.5 us (4%)
  between operations  13.2 us (3%)
  other arithmetic  12.2 us (3%)
    all_gather x1, waiting for transfers between devices, per_device(): lax.all_gather(qkv_weight, 'ctx', axis=1, tiled=True)  127 us
    reduce_scatter x1, waiting for transfers between devices, per_device(): lax.psum_scatter(lax.dot_general(mixed, out_rows, (((0,), (0,)), ((), ())...  74.5 us
    all_to_all x1, waiting for transfers between devices, per_device(): moved = lax.all_to_all(qkv, 'ctx', split_axis=1, concat_axis=2, tiled=True)  66.1 us
    all_to_all x1, waiting for transfers between devices, per_device(): lax.all_to_all(regrouped, 'ctx', split_axis=1, concat_axis=0, tiled=True)  15.2 us
    dot_general x1, matrix products, per_device(): jnp.einsum('tr,src->sct', tokens, lax.all_gather(qkv_weight, 'ctx', axis=...  14.8 us
    dot_general x1, matrix products, per_device(): lax.dot_general(mixed, out_rows, (((0,), (0,)), ((), ())), preferred_elem...  8.55 us
    all_gather x1, waiting for transfers between devices, per_device(): out_rows = lax.all_gather(out_weight, 'ctx', axis=1, tiled=True)  7.9 us
  transfers between devices with their start and end apart: 5, of which 5 were waited for; matrix products, arithmetic and copies ran while one was open for 7% of the time, Pallas kernels for 0%

commit v1 on v0

--- a/solution.py
+++ b/solution.py
@@ -2,6 +2,11 @@
 import jax.numpy as jnp
 from jax import lax
 from jax.sharding import PartitionSpec as P
+
+
+def all_by_exchange(x, axis, dim):
+    sent = jnp.stack([x] * lax.axis_size(axis))
+    return jnp.concatenate(lax.all_to_all(sent, axis, 0, 0), axis=dim)
 
 
 def short_conv(extended, short_filter):
@@ -56,7 +61,7 @@
     projected = jnp.einsum(
         "tr,src->sct",
         tokens,
-        lax.all_gather(qkv_weight, "ctx", axis=1, tiled=True),
+        all_by_exchange(qkv_weight, "ctx", 1),
         preferred_element_type=jnp.float32,
     )
     qkv = projected.astype(jnp.bfloat16)

time: 380 us -> 545 us (1.43)
  blocking collectives: 0 us -> 285 us
  waiting for transfers between devices: 291 us -> 163 us
  local copies, waits for them, and re-layouts: 20.7 us -> 28.4 us
    all_to_all x0 -> x1, blocking collectives: none -> 285 us  [all_by_exchange(): return jnp.concatenate(lax.all_to_all(sent, axis, 0, 0), axis=dim)]
    all_gather x1 -> x0, waiting for transfers between devices: 127 us -> none  [per_device(): lax.all_gather(qkv_weight, 'ctx', axis=1, tiled=True)]
    another operation x0 -> x1, local copies, waits for them, and re-layouts: none -> 7.62 us  [all_by_exchange(): sent = jnp.stack([x] * lax.axis_size(axis))]
    all_gather x1, waiting for transfers between devices: 7.9 us -> 1.19 us  [per_device(): out_rows = lax.all_gather(out_weight, 'ctx', axis=1, tiled=True)]
  transfers between devices with their start and end apart: 5 -> 4, of which waited for: 5 -> 4; matrix products, arithmetic and copies ran while one was open for 7% -> 5% of each run, Pallas kernels for 0% -> 0%
where the time goes in v1:
time: 545 us; the launch traced here: 544 us
  blocking collectives  285 us (52%)
  waiting for transfers between devices  163 us (30%)
  local copies, waits for them, and re-layouts  28.4 us (5%)
  matrix products  26.9 us (5%)
  other arithmetic  13.6 us (2%)
  between operations  13.6 us (2%)
  starting transfers between devices  13 us (2%)
    all_to_all x1, blocking collectives, all_by_exchange(): return jnp.concatenate(lax.all_to_all(sent, axis, 0, 0), axis=dim)  285 us
    reduce_scatter x1, waiting for transfers between devices, per_device(): lax.psum_scatter(lax.dot_general(mixed, out_rows, (((0,), (0,)), ((), ())...  77.1 us
    all_to_all x1, waiting for transfers between devices, per_device(): moved = lax.all_to_all(qkv, 'ctx', split_axis=1, concat_axis=2, tiled=True)  67.5 us
    all_to_all x1, waiting for transfers between devices, per_device(): lax.all_to_all(regrouped, 'ctx', split_axis=1, concat_axis=0, tiled=True)  17 us
    dot_general x1, matrix products, per_device(): jnp.einsum('tr,src->sct', tokens, all_by_exchange(qkv_weight, 'ctx', 1),...  13 us
  transfers between devices with their start and end apart: 4, of which 4 were waited for; matrix products, arithmetic and copies ran while one was open for 5% of the time, Pallas kernels for 0%

profile of v1, /device:TPU:1, one launch (start us, length us, event | category | flops | bytes accessed | tf_op | source)
XLA Modules:
  0.0 544.0 jit_solution(5288234366000196492)
XLA Ops:
  6.5 1.2 copy.14
  7.8 7.6 %stack.2 = bf16[32,3,128,512]{2,3,1,0:T(8,128)(2,1)} broadcast(bf16[3,128,512]{1,2,0:T(8,128)(2,1)S(1)} %copy.14), dimensions={1,2,3} | broadcast | bytes 12976128 | tf_op jit(solution)/shard_map/stack | solution.py:8
  15.4 285.2 %all_to_all.39 = bf16[32,3,128,512]{2,3,1,0:T(8,128)(2,1)S(1)} all-to-all(bf16[32,3,128,512]{2,3,1,0:T(8,128)(2,1)} %stack.2), channel_id=1, replica_groups=mesh['ctx'=32,'tp'=8] {'ctx'}, dimensions={0} | all-to-all | bytes 25165824 | tf_op jit(solution)/shard_map/all_to_all | solution.py:9
  300.6 13.0 %fusion.6 = bf16[3,512,768]{2,1,0:T(8,128)(2,1)} fusion(bf16[768,4096]{1,0:T(8,128)(2,1)} %param.7, bf16[32,3,128,512]{2,3,1,0:T(8,128)(2,1)S(1)} %all_to_all.39), kind=kOutput, calls=%fused_computation.13 | convolution fusion | flops 9664856064 | bytes 21233664 | tf_op jit(solution)/shard_map/tr,src->sct/dot_general | solution.py:61
  313.6 5.3 copy.16
  318.9 0.0 copy-start
  318.9 6.5 %all-to-all-start.1 = ((bf16[3,512,768]{2,0,1:T(4,128)(2,1)}), bf16[3,512,768]{2,0,1:T(4,128)(2,1)S(1)}, u32[]{:S(2)}, u32[]{:S(2)}) async-start(bf16[3,512,768]{2,0,1:T(4,128)(2,1)} %copy.16), calls=%async_computation.1 | async-start | bytes 6291456 | tf_op jit(solution)/shard_map/all_to_all | solution.py:72
  325.4 0.2 all-gather.2.cloned.1.call-start
  325.7 0.5 all-gather.2.cloned.1.call-update
  326.2 1.1 constant_dynamic-slice_fusion.5
  327.3 0.0 copy-done
  327.3 0.8 dynamic_slice.11
  328.1 0.6 dynamic-slice.7
  328.7 1.2 iota_compare_fusion
  330.0 3.5 fusion.3
  333.4 67.5 %all-to-all-done.1 = bf16[3,512,768]{2,0,1:T(4,128)(2,1)S(1)} async-done(((bf16[3,512,768]{2,0,1:T(4,128)(2,1)}), bf16[3,512,768]{2,0,1:T(4,128)(2,1)S(1)}, u32[]{:S(2)}, u32[]{:S(2)}) %all-to-all-start.1) | async-done | bytes 2359328 | tf_op jit(solution)/shard_map/all_to_all | solution.py:72
  400.9 3.1 copy.58
  404.0 3.0 all_to_all.32
  407.0 4.9 multiply_add_fusion
  411.9 0.2 fusion.11
  412.2 0.5 copy.31
  412.6 1.0 concatenate.7
  413.6 1.5 reshape.89
  415.1 0.4 fusion.13
  415.5 1.5 convolution_add_fusion
  417.0 2.6 reshape.93
  419.6 0.2 copy.32
  419.8 4.8 fusion.12
  424.6 6.3 %all-to-all-start.2 = ((bf16[16,32,768]{2,0,1:T(8,128)(2,1)}), bf16[16,32,768]{2,0,1:T(8,128)(2,1)S(1)}, u32[]{:S(2)}, u32[]{:S(2)}) async-start(bf16[16,32,768]{2,0,1:T(8,128)(2,1)} %fusion.12), calls=%async_computation.2 | async-start | bytes 1572864 | tf_op jit(solution)/shard_map/all_to_all | solution.py:85
  430.9 0.0 reduce-scatter.2.cloned.1.call-start
  430.9 1.2 all-gather.2.cloned.1.call-done
  432.1 17.0 %all-to-all-done.2 = bf16[16,32,768]{2,0,1:T(8,128)(2,1)S(1)} async-done(((bf16[16,32,768]{2,0,1:T(8,128)(2,1)}), bf16[16,32,768]{2,0,1:T(8,128)(2,1)S(1)}, u32[]{:S(2)}, u32[]{:S(2)}) %all-to-all-start.2) | async-done | bytes 786464 | tf_op jit(solution)/shard_map/all_to_all | solution.py:85
  449.1 8.5 %fusion.33 = f32[768,4096]{1,0:T(8,128)} fusion(bf16[512,768]{1,0:T(8,128)(2,1)S(1)} %bitcast.75, bf16[512,4096]{1,0:T(8,128)(2,1)} %all-gather.2.cloned.1.call-done), kind=kOutput, calls=%fused_computation.61 | convolution fusion | flops 3221225472 | bytes 17563648 | tf_op jit(solution)/shard_map/dot_general | solution.py:88
  457.6 0.0 reduce-scatter.2.cloned.1.call-update
  457.6 77.1 %reduce-scatter.2.cloned.1.call-done = f32[96,4096]{1,0:T(8,128)} async-done(((f32[768,4096]{1,0:T(8,128)}), f32[96,4096]{1,0:T(8,128)}) %reduce-scatter.2.cloned.1.call-update) | async-done | bytes 1572880 | tf_op jit(solution)/shard_map/reduce_scatter | solution.py:87
  534.8 2.4 convert_element_type.74
  (6 shorter events, 0.1 us)
Async XLA Ops:
  318.9 8.3 %copy-start = (f32[32]{0:T(128)S(1)}, f32[32]{0:T(128)}, u32[]{:S(2)}) copy-start(f32[32]{0:T(128)} %param.11) | copy-start | bytes 388
  318.9 82.0 %all-to-all-start.1 = ((bf16[3,512,768]{2,0,1:T(4,128)(2,1)}), bf16[3,512,768]{2,0,1:T(4,128)(2,1)S(1)}, u32[]{:S(2)}, u32[]{:S(2)}) async-start(bf16[3,512,768]{2,0,1:T(4,128)(2,1)} %copy.16), calls=%async_computation.1 | async-start | bytes 6291456 | tf_op jit(solution)/shard_map/all_to_all | solution.py:72
  325.4 106.7 %all-gather.2.cloned.1.call-start = ((), (), s32[]{:S(2)}) async-start(), calls=%async_computation.4 | async-start | bytes 4325376 | tf_op jit(solution)/shard_map/all_gather | solution.py:86
  424.6 24.5 %all-to-all-start.2 = ((bf16[16,32,768]{2,0,1:T(8,128)(2,1)}), bf16[16,32,768]{2,0,1:T(8,128)(2,1)S(1)}, u32[]{:S(2)}, u32[]{:S(2)}) async-start(bf16[16,32,768]{2,0,1:T(8,128)(2,1)} %fusion.12), calls=%async_computation.2 | async-start | bytes 1572864 | tf_op jit(solution)/shard_map/all_to_all | solution.py:85
  430.9 103.9 %reduce-scatter.2.cloned.1.call-start = ((), (), s32[]{:S(2)}) async-start(), calls=%async_computation.5 | async-start | bytes 14155776 | tf_op jit(solution)/shard_map/reduce_scatter | solution.py:87
Sparse Core Ops, SparseCore 0:
  328.7 103.3 all-gather.1
  457.8 76.9 reduce-scatter.1
